TPU v7x, 256 devices: a whole 4x4x8 slice. The times are simulated.
256 devices in a mesh: section: 8 (over x, core), expert: 32 (over y, z).
Axes of the slice: x: 4, y: 4, z: 8, core: 2. Of those that a mesh axis runs over, the one named last changes fastest.
Arguments:
- tokens: bfloat16 [2, 512, 2048], P(None, 'expert'), may hold values from -6 to 6
- norm_gain: float32 [8, 2048], P('section'), may hold values from 0.1 to 1.9
- w_gate: bfloat16 [8, 2048, 24576], P('section', None, 'expert'), may hold values from -0.125 to 0.125
- w_up: bfloat16 [8, 2048, 24576], P('section', None, 'expert'), may hold values from -0.125 to 0.125
- w_down: bfloat16 [8, 24576, 2048], P('section', 'expert'), may hold values from -0.15625 to 0.15625
- routes: int32 [8, 2, 512, 2], P('section', None, 'expert'), may hold values from 0 to 15, all different within a row; in each aligned block of 16 rows (0 to 15, 16 to 31, ..., all dimensions but the last counted through in order) at most 4 rows name the same one
- route_weights: float32 [8, 2, 512, 2], P('section', None, 'expert'), may hold values from 0.25 to 1
Outputs:
- hidden: bfloat16 [8, 2, 512, 2048], P('section', None, 'expert')
Inputs may be any that keep to these rules, and one draw needn't show every extreme that they name: `routes`: each token names 2 different experts. Within the tokens of one device (aligned blocks of 16 rows, for every layer and micro-batch), no expert is named by more than 4 of the token choices, and in some blocks one expert by exactly 4.
All inputs are finite; a program needn't handle non-finite values.
Results may differ from a plain program's by a relative error of at most 0.025.
Values may be sent and summed in bfloat16 or wider, within the bound.
A program may use at most 64 MiB of HBM per device.

v0:
```python
import jax
import jax.numpy as jnp
from jax import lax
from jax.sharding import PartitionSpec as P


def shifted(shard, axis, by):
    count = lax.axis_size(axis)
    pairs = [(i, i + by) for i in range(count) if 0 <= i + by < count]
    return lax.ppermute(shard, axis, pairs)


def normalize(layer_in, gain_row):
    wide_input = layer_in.astype(jnp.float32)
    inv_rms = lax.rsqrt(jnp.mean(wide_input * wide_input, axis=-1, keepdims=True) + 1e-06)
    return (wide_input, (wide_input * inv_rms * gain_row).astype(jnp.bfloat16))


def expert_rows(arrived, gate_cols, up_cols, down_rows):
    flat_rows = arrived.reshape(-1, arrived.shape[-1])
    gate_act = jnp.dot(flat_rows, gate_cols, preferred_element_type=jnp.float32)
    up_act = jnp.dot(flat_rows, up_cols, preferred_element_type=jnp.float32)
    product = (jax.nn.silu(gate_act) * up_act).astype(jnp.bfloat16)
    partial_value = jnp.dot(product, down_rows, preferred_element_type=jnp.float32).astype(
        jnp.bfloat16
    )
    return partial_value.reshape(arrived.shape)


def return_rows(partial_value):
    return lax.all_to_all(partial_value, "expert", split_axis=0, concat_axis=0, tiled=True)


def on_device(tokens, norm_gain, w_gate, w_up, w_down, routes, route_weights):
    micro_count, tok_rows, model_dim = tokens.shape
    fanout = routes.shape[-1]
    sections = lax.axis_size("section")
    devices = lax.axis_size("expert")
    experts = devices // 2
    capacity = min(tok_rows, 2 * tok_rows * fanout // experts)
    section_idx = lax.axis_index("section")
    gate_cols = w_gate[0]
    up_cols = w_up[0]
    down_rows = w_down[0]
    gain_row = norm_gain[0]
    slot_ids = jnp.arange(experts * capacity, dtype=jnp.int32)

    def run_layer(layer_in, picked, weights):
        wide_input, normed = normalize(layer_in, gain_row)
        choices = picked.reshape(-1)
        onehot = (choices[:, None] == jnp.arange(experts, dtype=jnp.int32)[None, :]).astype(
            jnp.int32
        )
        earlier = jnp.cumsum(onehot, axis=0) - onehot
        slot_idx = jnp.sum(earlier * onehot, axis=1)
        position = (choices * capacity + slot_idx).reshape(tok_rows, fanout)
        matches = slot_ids[None, None, :] == position[:, :, None]
        dispatch_map = jnp.sum(matches.astype(jnp.float32), axis=1).astype(jnp.bfloat16)
        packed = jnp.dot(dispatch_map.T, normed, preferred_element_type=jnp.float32).astype(
            jnp.bfloat16
        )
        packed = packed.reshape(experts, capacity, model_dim)
        mixing = jnp.sum(jnp.where(matches, weights[:, :, None], 0.0), axis=1)
        copies = jnp.broadcast_to(packed[:, None], (experts, 2, capacity, model_dim)).reshape(
            devices, capacity, model_dim
        )
        returned = (
            lambda arrived: return_rows(expert_rows(arrived, gate_cols, up_cols, down_rows))
        )(lax.all_to_all(copies, "expert", split_axis=0, concat_axis=0, tiled=True))
        summed = jnp.sum(
            returned.reshape(experts, 2, capacity, model_dim).astype(jnp.float32), axis=1
        ).astype(jnp.bfloat16)
        summed = summed.astype(jnp.float32).reshape(experts * capacity, model_dim)
        output = wide_input + jnp.dot(
            mixing, summed, precision=lax.Precision.HIGHEST, preferred_element_type=jnp.float32
        )
        return output.astype(jnp.bfloat16)

    def advance(step_idx, loop_state):
        handed, hidden = loop_state
        micro_pos = step_idx - section_idx
        micro_idx = jnp.clip(micro_pos, 0, micro_count - 1)
        first_rows = lax.dynamic_index_in_dim(
            tokens, jnp.minimum(step_idx, micro_count - 1), 0, keepdims=False
        )
        layer_in = jnp.where(section_idx == 0, first_rows, handed)
        picked = lax.dynamic_index_in_dim(routes[0], micro_idx, 0, keepdims=False)
        weights = lax.dynamic_index_in_dim(route_weights[0], micro_idx, 0, keepdims=False)
        result = run_layer(layer_in, picked, weights)
        active = (micro_pos >= 0) & (micro_pos < micro_count)
        current = lax.dynamic_index_in_dim(hidden[0], micro_idx, 0, keepdims=False)
        stored = jnp.where(active, result, current)
        hidden = lax.dynamic_update_slice(hidden, stored[None, None], (0, micro_idx, 0, 0))
        handed = shifted(result, "section", 1)
        return (handed, hidden)

    initial = (
        jnp.zeros((tok_rows, model_dim), jnp.bfloat16),
        jnp.zeros((1, micro_count, tok_rows, model_dim), jnp.bfloat16),
    )
    return lax.fori_loop(0, micro_count + sections - 1, advance, initial)[1]


def solution(mesh):
    in_specs = (
        P(None, "expert", None),
        P("section", None),
        P("section", None, "expert"),
        P("section", None, "expert"),
        P("section", "expert", None),
        P("section", None, "expert", None),
        P("section", None, "expert", None),
    )
    out_specs = P("section", None, "expert", None)
    return jax.shard_map(
        on_device, mesh=mesh, in_specs=in_specs, out_specs=out_specs, check_vma=False
    )
```

profile of v0, /device:TPU:1, one launch (start us, length us, event | category | flops | bytes accessed | tf_op | source)
XLA Modules:
  0.0 592.6 jit_solution(1712548634614921293)
XLA Ops:
  0.7 591.9 %while.18 = (s32[]{:T(128)}, bf16[16,2048]{1,0:T(8,128)(2,1)S(1)}, bf16[1,2,16,2048]{3,2,1,0:T(8,128)(2,1)}, pred[]{:T(512)}, bf16[2,16,2048]{2,1,0:T(8,128)(2,1...) while((s32[]{:T(128)}, bf16[16,2048]{1,0:T(8,128)(2,1)S(1)}, ...), condition=%wide.region_7.8_spmd.clone, body=%wide.region_0.7_spmd.clone.sunk | while | flops 1238854656 | bytes 34245804 | solution.py:101
  7.6 26.5 %all_to_all.28 = bf16[32,4,2048]{2,1,0:T(4,128)(2,1)} all-to-all(bf16[32,4,2048]{2,1,0:T(4,128)(2,1)S(1)} %bitcast.61), channel_id=1, replica_groups=mesh['section'=8,'expert'=32] {'expert'}, dimensions={0} | all-to-all | bytes 1048576 | tf_op jit(solution)/shard_map/while/body/eval_jaxpr/all_to_all | solution.py:69
  34.1 1.9 reshape.111
  36.0 2.4 fusion.60
  38.4 4.4 convolution_convert_fusion.5
  43.8 7.2 %all-to-all-start.1 = ((bf16[32,4,2048]{2,1,0:T(4,128)(2,1)}), bf16[32,4,2048]{2,1,0:T(4,128)(2,1)S(1)}, u32[]{:S(2)}, u32[]{:S(2)}) async-start(bf16[32,4,2048]{2,1,0:T(4,128)(2,1)} %reshape.112), calls=%async_computation.1 | async-start | bytes 1048576 | tf_op jit(solution)/shard_map/while/body/eval_jaxpr/all_to_all | solution.py:31
  51.1 13.8 %all-to-all-done.1 = bf16[32,4,2048]{2,1,0:T(4,128)(2,1)S(1)} async-done(((bf16[32,4,2048]{2,1,0:T(4,128)(2,1)}), bf16[32,4,2048]{2,1,0:T(4,128)(2,1)S(1)}, u32[]{:S(2)}, u32[]{:S(2)}) %all-to-all-start.1) | async-done | bytes 524320 | tf_op jit(solution)/shard_map/while/body/eval_jaxpr/all_to_all | solution.py:31
  65.5 7.4 %collective-permute-start = (bf16[16,2048]{1,0:T(8,128)(2,1)S(1)}, bf16[16,2048]{1,0:T(8,128)(2,1)S(1)}, u32[]{:S(2)}, u32[]{:S(2)}) collective-permute-start(bf16[16,2048]{1,0:T(8,128)(2,1)S(1)} %get-tuple-element.473), channel_id=1, source_target_pairs={{0,32},{32,64},{64,96},{96,128},{128,160},{160,192},{192,224},{1,3... | collective-permute-start | bytes 196616 | tf_op jit(solution)/shard_map/while/body/eval_jaxpr/ppermute | solution.py:10
  81.1 20.5 %all_to_all.28 = bf16[32,4,2048]{2,1,0:T(4,128)(2,1)} all-to-all(bf16[32,4,2048]{2,1,0:T(4,128)(2,1)S(1)} %bitcast.61), channel_id=1, replica_groups=mesh['section'=8,'expert'=32] {'expert'}, dimensions={0} | all-to-all | bytes 1048576 | tf_op jit(solution)/shard_map/while/body/eval_jaxpr/all_to_all | solution.py:69
  101.6 1.9 reshape.111
  103.5 2.4 fusion.60
  105.9 4.4 convolution_convert_fusion.5
  111.3 5.5 all-to-all-start.1
  116.8 14.8 %all-to-all-done.1 = bf16[32,4,2048]{2,1,0:T(4,128)(2,1)S(1)} async-done(((bf16[32,4,2048]{2,1,0:T(4,128)(2,1)}), bf16[32,4,2048]{2,1,0:T(4,128)(2,1)S(1)}, u32[]{:S(2)}, u32[]{:S(2)}) %all-to-all-start.1) | async-done | bytes 524320 | tf_op jit(solution)/shard_map/while/body/eval_jaxpr/all_to_all | solution.py:31
  132.3 7.0 %collective-permute-start = (bf16[16,2048]{1,0:T(8,128)(2,1)S(1)}, bf16[16,2048]{1,0:T(8,128)(2,1)S(1)}, u32[]{:S(2)}, u32[]{:S(2)}) collective-permute-start(bf16[16,2048]{1,0:T(8,128)(2,1)S(1)} %get-tuple-element.473), channel_id=1, source_target_pairs={{0,32},{32,64},{64,96},{96,128},{128,160},{160,192},{192,224},{1,3... | collective-permute-start | bytes 196616 | tf_op jit(solution)/shard_map/while/body/eval_jaxpr/ppermute | solution.py:10
  147.5 20.2 %all_to_all.28 = bf16[32,4,2048]{2,1,0:T(4,128)(2,1)} all-to-all(bf16[32,4,2048]{2,1,0:T(4,128)(2,1)S(1)} %bitcast.61), channel_id=1, replica_groups=mesh['section'=8,'expert'=32] {'expert'}, dimensions={0} | all-to-all | bytes 1048576 | tf_op jit(solution)/shard_map/while/body/eval_jaxpr/all_to_all | solution.py:69
  167.7 1.9 reshape.111
  169.7 2.4 fusion.60
  172.1 4.4 convolution_convert_fusion.5
  177.5 5.2 all-to-all-start.1
  182.7 14.9 %all-to-all-done.1 = bf16[32,4,2048]{2,1,0:T(4,128)(2,1)S(1)} async-done(((bf16[32,4,2048]{2,1,0:T(4,128)(2,1)}), bf16[32,4,2048]{2,1,0:T(4,128)(2,1)S(1)}, u32[]{:S(2)}, u32[]{:S(2)}) %all-to-all-start.1) | async-done | bytes 524320 | tf_op jit(solution)/shard_map/while/body/eval_jaxpr/all_to_all | solution.py:31
  198.3 6.6 %collective-permute-start = (bf16[16,2048]{1,0:T(8,128)(2,1)S(1)}, bf16[16,2048]{1,0:T(8,128)(2,1)S(1)}, u32[]{:S(2)}, u32[]{:S(2)}) collective-permute-start(bf16[16,2048]{1,0:T(8,128)(2,1)S(1)} %get-tuple-element.473), channel_id=1, source_target_pairs={{0,32},{32,64},{64,96},{96,128},{128,160},{160,192},{192,224},{1,3... | collective-permute-start | bytes 196616 | tf_op jit(solution)/shard_map/while/body/eval_jaxpr/ppermute | solution.py:10
  213.1 20.4 %all_to_all.28 = bf16[32,4,2048]{2,1,0:T(4,128)(2,1)} all-to-all(bf16[32,4,2048]{2,1,0:T(4,128)(2,1)S(1)} %bitcast.61), channel_id=1, replica_groups=mesh['section'=8,'expert'=32] {'expert'}, dimensions={0} | all-to-all | bytes 1048576 | tf_op jit(solution)/shard_map/while/body/eval_jaxpr/all_to_all | solution.py:69
  233.5 1.9 reshape.111
  235.4 2.4 fusion.60
  237.8 4.4 convolution_convert_fusion.5
  243.2 5.5 all-to-all-start.1
  248.7 14.8 %all-to-all-done.1 = bf16[32,4,2048]{2,1,0:T(4,128)(2,1)S(1)} async-done(((bf16[32,4,2048]{2,1,0:T(4,128)(2,1)}), bf16[32,4,2048]{2,1,0:T(4,128)(2,1)S(1)}, u32[]{:S(2)}, u32[]{:S(2)}) %all-to-all-start.1) | async-done | bytes 524320 | tf_op jit(solution)/shard_map/while/body/eval_jaxpr/all_to_all | solution.py:31
  264.2 3.2 collective-permute-start
  276.0 20.5 %all_to_all.28 = bf16[32,4,2048]{2,1,0:T(4,128)(2,1)} all-to-all(bf16[32,4,2048]{2,1,0:T(4,128)(2,1)S(1)} %bitcast.61), channel_id=1, replica_groups=mesh['section'=8,'expert'=32] {'expert'}, dimensions={0} | all-to-all | bytes 1048576 | tf_op jit(solution)/shard_map/while/body/eval_jaxpr/all_to_all | solution.py:69
  296.5 1.9 reshape.111
  298.5 2.4 fusion.60
  300.8 4.4 convolution_convert_fusion.5
  306.2 7.4 %all-to-all-start.1 = ((bf16[32,4,2048]{2,1,0:T(4,128)(2,1)}), bf16[32,4,2048]{2,1,0:T(4,128)(2,1)S(1)}, u32[]{:S(2)}, u32[]{:S(2)}) async-start(bf16[32,4,2048]{2,1,0:T(4,128)(2,1)} %reshape.112), calls=%async_computation.1 | async-start | bytes 1048576 | tf_op jit(solution)/shard_map/while/body/eval_jaxpr/all_to_all | solution.py:31
  313.7 14.5 %all-to-all-done.1 = bf16[32,4,2048]{2,1,0:T(4,128)(2,1)S(1)} async-done(((bf16[32,4,2048]{2,1,0:T(4,128)(2,1)}), bf16[32,4,2048]{2,1,0:T(4,128)(2,1)S(1)}, u32[]{:S(2)}, u32[]{:S(2)}) %all-to-all-start.1) | async-done | bytes 524320 | tf_op jit(solution)/shard_map/while/body/eval_jaxpr/all_to_all | solution.py:31
  330.8 3.2 collective-permute-done
  340.9 20.1 %all_to_all.28 = bf16[32,4,2048]{2,1,0:T(4,128)(2,1)} all-to-all(bf16[32,4,2048]{2,1,0:T(4,128)(2,1)S(1)} %bitcast.61), channel_id=1, replica_groups=mesh['section'=8,'expert'=32] {'expert'}, dimensions={0} | all-to-all | bytes 1048576 | tf_op jit(solution)/shard_map/while/body/eval_jaxpr/all_to_all | solution.py:69
  361.0 1.9 reshape.111
  362.9 2.4 fusion.60
  365.3 4.4 convolution_convert_fusion.5
  370.7 7.5 %all-to-all-start.1 = ((bf16[32,4,2048]{2,1,0:T(4,128)(2,1)}), bf16[32,4,2048]{2,1,0:T(4,128)(2,1)S(1)}, u32[]{:S(2)}, u32[]{:S(2)}) async-start(bf16[32,4,2048]{2,1,0:T(4,128)(2,1)} %reshape.112), calls=%async_computation.1 | async-start | bytes 1048576 | tf_op jit(solution)/shard_map/while/body/eval_jaxpr/all_to_all | solution.py:31
  378.3 14.5 %all-to-all-done.1 = bf16[32,4,2048]{2,1,0:T(4,128)(2,1)S(1)} async-done(((bf16[32,4,2048]{2,1,0:T(4,128)(2,1)}), bf16[32,4,2048]{2,1,0:T(4,128)(2,1)S(1)}, u32[]{:S(2)}, u32[]{:S(2)}) %all-to-all-start.1) | async-done | bytes 524320 | tf_op jit(solution)/shard_map/while/body/eval_jaxpr/all_to_all | solution.py:31
  395.4 3.2 collective-permute-done
  405.5 20.1 %all_to_all.28 = bf16[32,4,2048]{2,1,0:T(4,128)(2,1)} all-to-all(bf16[32,4,2048]{2,1,0:T(4,128)(2,1)S(1)} %bitcast.61), channel_id=1, replica_groups=mesh['section'=8,'expert'=32] {'expert'}, dimensions={0} | all-to-all | bytes 1048576 | tf_op jit(solution)/shard_map/while/body/eval_jaxpr/all_to_all | solution.py:69
  425.6 1.9 reshape.111
  427.6 2.4 fusion.60
  430.0 4.4 convolution_convert_fusion.5
  435.4 7.6 %all-to-all-start.1 = ((bf16[32,4,2048]{2,1,0:T(4,128)(2,1)}), bf16[32,4,2048]{2,1,0:T(4,128)(2,1)S(1)}, u32[]{:S(2)}, u32[]{:S(2)}) async-start(bf16[32,4,2048]{2,1,0:T(4,128)(2,1)} %reshape.112), calls=%async_computation.1 | async-start | bytes 1048576 | tf_op jit(solution)/shard_map/while/body/eval_jaxpr/all_to_all | solution.py:31
  443.0 14.5 %all-to-all-done.1 = bf16[32,4,2048]{2,1,0:T(4,128)(2,1)S(1)} async-done(((bf16[32,4,2048]{2,1,0:T(4,128)(2,1)}), bf16[32,4,2048]{2,1,0:T(4,128)(2,1)S(1)}, u32[]{:S(2)}, u32[]{:S(2)}) %all-to-all-start.1) | async-done | bytes 524320 | tf_op jit(solution)/shard_map/while/body/eval_jaxpr/all_to_all | solution.py:31
  460.1 3.2 collective-permute-done
  470.2 20.1 %all_to_all.28 = bf16[32,4,2048]{2,1,0:T(4,128)(2,1)} all-to-all(bf16[32,4,2048]{2,1,0:T(4,128)(2,1)S(1)} %bitcast.61), channel_id=1, replica_groups=mesh['section'=8,'expert'=32] {'expert'}, dimensions={0} | all-to-all | bytes 1048576 | tf_op jit(solution)/shard_map/while/body/eval_jaxpr/all_to_all | solution.py:69
  490.3 1.9 reshape.111
  492.3 2.4 fusion.60
  494.6 4.4 convolution_convert_fusion.5
  500.0 7.5 %all-to-all-start.1 = ((bf16[32,4,2048]{2,1,0:T(4,128)(2,1)}), bf16[32,4,2048]{2,1,0:T(4,128)(2,1)S(1)}, u32[]{:S(2)}, u32[]{:S(2)}) async-start(bf16[32,4,2048]{2,1,0:T(4,128)(2,1)} %reshape.112), calls=%async_computation.1 | async-start | bytes 1048576 | tf_op jit(solution)/shard_map/while/body/eval_jaxpr/all_to_all | solution.py:31
  507.6 14.5 %all-to-all-done.1 = bf16[32,4,2048]{2,1,0:T(4,128)(2,1)S(1)} async-done(((bf16[32,4,2048]{2,1,0:T(4,128)(2,1)}), bf16[32,4,2048]{2,1,0:T(4,128)(2,1)S(1)}, u32[]{:S(2)}, u32[]{:S(2)}) %all-to-all-start.1) | async-done | bytes 524320 | tf_op jit(solution)/shard_map/while/body/eval_jaxpr/all_to_all | solution.py:31
  524.7 3.2 collective-permute-done
  534.9 20.1 %all_to_all.28 = bf16[32,4,2048]{2,1,0:T(4,128)(2,1)} all-to-all(bf16[32,4,2048]{2,1,0:T(4,128)(2,1)S(1)} %bitcast.61), channel_id=1, replica_groups=mesh['section'=8,'expert'=32] {'expert'}, dimensions={0} | all-to-all | bytes 1048576 | tf_op jit(solution)/shard_map/while/body/eval_jaxpr/all_to_all | solution.py:69
  555.0 1.9 reshape.111
  556.9 2.4 fusion.60
  559.3 4.4 convolution_convert_fusion.5
  564.7 7.5 %all-to-all-start.1 = ((bf16[32,4,2048]{2,1,0:T(4,128)(2,1)}), bf16[32,4,2048]{2,1,0:T(4,128)(2,1)S(1)}, u32[]{:S(2)}, u32[]{:S(2)}) async-start(bf16[32,4,2048]{2,1,0:T(4,128)(2,1)} %reshape.112), calls=%async_computation.1 | async-start | bytes 1048576 | tf_op jit(solution)/shard_map/while/body/eval_jaxpr/all_to_all | solution.py:31
  572.3 14.5 %all-to-all-done.1 = bf16[32,4,2048]{2,1,0:T(4,128)(2,1)S(1)} async-done(((bf16[32,4,2048]{2,1,0:T(4,128)(2,1)}), bf16[32,4,2048]{2,1,0:T(4,128)(2,1)S(1)}, u32[]{:S(2)}, u32[]{:S(2)}) %all-to-all-start.1) | async-done | bytes 524320 | tf_op jit(solution)/shard_map/while/body/eval_jaxpr/all_to_all | solution.py:31
  589.4 3.2 collective-permute-done
  (254 shorter events, 92.5 us)
Async XLA Ops:
  0.7 35.3 %copy-start = (bf16[2048,768]{1,0:T(8,128)(2,1)S(1)}, bf16[2048,768]{1,0:T(8,128)(2,1)}, u32[]{:S(2)}) copy-start(bf16[2048,768]{1,0:T(8,128)(2,1)} %get-tuple-element.514) | copy-start | bytes 9437188 | tf_op jit(solution)/shard_map/while
  38.4 12.7 %copy-start.1 = (bf16[1,2,16,2048]{3,2,1,0:T(8,128)(2,1)S(1)}, bf16[1,2,16,2048]{3,2,1,0:T(8,128)(2,1)}, u32[]{:S(2)}) copy-start(bf16[1,2,16,2048]{3,2,1,0:T(8,128)(2,1)} %get-tuple-element.492) | copy-start | bytes 393220 | tf_op jit(solution)/shard_map/while
  43.8 21.0 %all-to-all-start.1 = ((bf16[32,4,2048]{2,1,0:T(4,128)(2,1)}), bf16[32,4,2048]{2,1,0:T(4,128)(2,1)S(1)}, u32[]{:S(2)}, u32[]{:S(2)}) async-start(bf16[32,4,2048]{2,1,0:T(4,128)(2,1)} %reshape.112), calls=%async_computation.1 | async-start | bytes 1048576 | tf_op jit(solution)/shard_map/while/body/eval_jaxpr/all_to_all | solution.py:31
  65.5 8.7 %copy-start.2 = (bf16[1,2,16,2048]{3,2,1,0:T(8,128)(2,1)}, bf16[1,2,16,2048]{3,2,1,0:T(8,128)(2,1)S(1)}, u32[]{:S(2)}) copy-start(bf16[1,2,16,2048]{3,2,1,0:T(8,128)(2,1)S(1)} %get-tuple-element.507) | copy-start | bytes 393220 | tf_op jit(solution)/shard_map/while
  65.5 8.7 %collective-permute-start = (bf16[16,2048]{1,0:T(8,128)(2,1)S(1)}, bf16[16,2048]{1,0:T(8,128)(2,1)S(1)}, u32[]{:S(2)}, u32[]{:S(2)}) collective-permute-start(bf16[16,2048]{1,0:T(8,128)(2,1)S(1)} %get-tuple-element.473), channel_id=1, source_target_pairs={{0,32},{32,64},{64,96},{96,128},{128,160},{160,192},{192,224},{1,3... | collective-permute-start | bytes 196616 | tf_op jit(solution)/shard_map/while/body/eval_jaxpr/ppermute | solution.py:10
  74.2 29.3 %copy-start = (bf16[2048,768]{1,0:T(8,128)(2,1)S(1)}, bf16[2048,768]{1,0:T(8,128)(2,1)}, u32[]{:S(2)}) copy-start(bf16[2048,768]{1,0:T(8,128)(2,1)} %get-tuple-element.514) | copy-start | bytes 9437188 | tf_op jit(solution)/shard_map/while
  105.9 10.9 %copy-start.1 = (bf16[1,2,16,2048]{3,2,1,0:T(8,128)(2,1)S(1)}, bf16[1,2,16,2048]{3,2,1,0:T(8,128)(2,1)}, u32[]{:S(2)}) copy-start(bf16[1,2,16,2048]{3,2,1,0:T(8,128)(2,1)} %get-tuple-element.492) | copy-start | bytes 393220 | tf_op jit(solution)/shard_map/while
  111.3 20.4 %all-to-all-start.1 = ((bf16[32,4,2048]{2,1,0:T(4,128)(2,1)}), bf16[32,4,2048]{2,1,0:T(4,128)(2,1)S(1)}, u32[]{:S(2)}, u32[]{:S(2)}) async-start(bf16[32,4,2048]{2,1,0:T(4,128)(2,1)} %reshape.112), calls=%async_computation.1 | async-start | bytes 1048576 | tf_op jit(solution)/shard_map/while/body/eval_jaxpr/all_to_all | solution.py:31
  132.3 8.3 %copy-start.2 = (bf16[1,2,16,2048]{3,2,1,0:T(8,128)(2,1)}, bf16[1,2,16,2048]{3,2,1,0:T(8,128)(2,1)S(1)}, u32[]{:S(2)}) copy-start(bf16[1,2,16,2048]{3,2,1,0:T(8,128)(2,1)S(1)} %get-tuple-element.507) | copy-start | bytes 393220 | tf_op jit(solution)/shard_map/while
  132.3 8.3 %collective-permute-start = (bf16[16,2048]{1,0:T(8,128)(2,1)S(1)}, bf16[16,2048]{1,0:T(8,128)(2,1)S(1)}, u32[]{:S(2)}, u32[]{:S(2)}) collective-permute-start(bf16[16,2048]{1,0:T(8,128)(2,1)S(1)} %get-tuple-element.473), channel_id=1, source_target_pairs={{0,32},{32,64},{64,96},{96,128},{128,160},{160,192},{192,224},{1,3... | collective-permute-start | bytes 196616 | tf_op jit(solution)/shard_map/while/body/eval_jaxpr/ppermute | solution.py:10
  140.6 29.1 %copy-start = (bf16[2048,768]{1,0:T(8,128)(2,1)S(1)}, bf16[2048,768]{1,0:T(8,128)(2,1)}, u32[]{:S(2)}) copy-start(bf16[2048,768]{1,0:T(8,128)(2,1)} %get-tuple-element.514) | copy-start | bytes 9437188 | tf_op jit(solution)/shard_map/while
  172.1 10.6 %copy-start.1 = (bf16[1,2,16,2048]{3,2,1,0:T(8,128)(2,1)S(1)}, bf16[1,2,16,2048]{3,2,1,0:T(8,128)(2,1)}, u32[]{:S(2)}) copy-start(bf16[1,2,16,2048]{3,2,1,0:T(8,128)(2,1)} %get-tuple-element.492) | copy-start | bytes 393220 | tf_op jit(solution)/shard_map/while
  177.5 20.1 %all-to-all-start.1 = ((bf16[32,4,2048]{2,1,0:T(4,128)(2,1)}), bf16[32,4,2048]{2,1,0:T(4,128)(2,1)S(1)}, u32[]{:S(2)}, u32[]{:S(2)}) async-start(bf16[32,4,2048]{2,1,0:T(4,128)(2,1)} %reshape.112), calls=%async_computation.1 | async-start | bytes 1048576 | tf_op jit(solution)/shard_map/while/body/eval_jaxpr/all_to_all | solution.py:31
  198.2 7.9 %copy-start.2 = (bf16[1,2,16,2048]{3,2,1,0:T(8,128)(2,1)}, bf16[1,2,16,2048]{3,2,1,0:T(8,128)(2,1)S(1)}, u32[]{:S(2)}) copy-start(bf16[1,2,16,2048]{3,2,1,0:T(8,128)(2,1)S(1)} %get-tuple-element.507) | copy-start | bytes 393220 | tf_op jit(solution)/shard_map/while
  198.3 7.9 %collective-permute-start = (bf16[16,2048]{1,0:T(8,128)(2,1)S(1)}, bf16[16,2048]{1,0:T(8,128)(2,1)S(1)}, u32[]{:S(2)}, u32[]{:S(2)}) collective-permute-start(bf16[16,2048]{1,0:T(8,128)(2,1)S(1)} %get-tuple-element.473), channel_id=1, source_target_pairs={{0,32},{32,64},{64,96},{96,128},{128,160},{160,192},{192,224},{1,3... | collective-permute-start | bytes 196616 | tf_op jit(solution)/shard_map/while/body/eval_jaxpr/ppermute | solution.py:10
  206.1 29.3 %copy-start = (bf16[2048,768]{1,0:T(8,128)(2,1)S(1)}, bf16[2048,768]{1,0:T(8,128)(2,1)}, u32[]{:S(2)}) copy-start(bf16[2048,768]{1,0:T(8,128)(2,1)} %get-tuple-element.514) | copy-start | bytes 9437188 | tf_op jit(solution)/shard_map/while
  237.8 10.9 %copy-start.1 = (bf16[1,2,16,2048]{3,2,1,0:T(8,128)(2,1)S(1)}, bf16[1,2,16,2048]{3,2,1,0:T(8,128)(2,1)}, u32[]{:S(2)}) copy-start(bf16[1,2,16,2048]{3,2,1,0:T(8,128)(2,1)} %get-tuple-element.492) | copy-start | bytes 393220 | tf_op jit(solution)/shard_map/while
  243.2 20.3 %all-to-all-start.1 = ((bf16[32,4,2048]{2,1,0:T(4,128)(2,1)}), bf16[32,4,2048]{2,1,0:T(4,128)(2,1)S(1)}, u32[]{:S(2)}, u32[]{:S(2)}) async-start(bf16[32,4,2048]{2,1,0:T(4,128)(2,1)} %reshape.112), calls=%async_computation.1 | async-start | bytes 1048576 | tf_op jit(solution)/shard_map/while/body/eval_jaxpr/all_to_all | solution.py:31
  264.2 5.0 copy-start.2
  264.2 4.9 collective-permute-start
  269.1 29.3 %copy-start = (bf16[2048,768]{1,0:T(8,128)(2,1)S(1)}, bf16[2048,768]{1,0:T(8,128)(2,1)}, u32[]{:S(2)}) copy-start(bf16[2048,768]{1,0:T(8,128)(2,1)} %get-tuple-element.514) | copy-start | bytes 9437188 | tf_op jit(solution)/shard_map/while
  300.8 12.8 %copy-start.1 = (bf16[1,2,16,2048]{3,2,1,0:T(8,128)(2,1)S(1)}, bf16[1,2,16,2048]{3,2,1,0:T(8,128)(2,1)}, u32[]{:S(2)}) copy-start(bf16[1,2,16,2048]{3,2,1,0:T(8,128)(2,1)} %get-tuple-element.492) | copy-start | bytes 393220 | tf_op jit(solution)/shard_map/while
  306.2 22.0 %all-to-all-start.1 = ((bf16[32,4,2048]{2,1,0:T(4,128)(2,1)}), bf16[32,4,2048]{2,1,0:T(4,128)(2,1)S(1)}, u32[]{:S(2)}, u32[]{:S(2)}) async-start(bf16[32,4,2048]{2,1,0:T(4,128)(2,1)} %reshape.112), calls=%async_computation.1 | async-start | bytes 1048576 | tf_op jit(solution)/shard_map/while/body/eval_jaxpr/all_to_all | solution.py:31
  328.8 5.1 copy-start.2
  328.9 5.1 collective-permute-start
  334.0 29.0 %copy-start = (bf16[2048,768]{1,0:T(8,128)(2,1)S(1)}, bf16[2048,768]{1,0:T(8,128)(2,1)}, u32[]{:S(2)}) copy-start(bf16[2048,768]{1,0:T(8,128)(2,1)} %get-tuple-element.514) | copy-start | bytes 9437188 | tf_op jit(solution)/shard_map/while
  365.3 13.0 %copy-start.1 = (bf16[1,2,16,2048]{3,2,1,0:T(8,128)(2,1)S(1)}, bf16[1,2,16,2048]{3,2,1,0:T(8,128)(2,1)}, u32[]{:S(2)}) copy-start(bf16[1,2,16,2048]{3,2,1,0:T(8,128)(2,1)} %get-tuple-element.492) | copy-start | bytes 393220 | tf_op jit(solution)/shard_map/while
  370.7 22.1 %all-to-all-start.1 = ((bf16[32,4,2048]{2,1,0:T(4,128)(2,1)}), bf16[32,4,2048]{2,1,0:T(4,128)(2,1)S(1)}, u32[]{:S(2)}, u32[]{:S(2)}) async-start(bf16[32,4,2048]{2,1,0:T(4,128)(2,1)} %reshape.112), calls=%async_computation.1 | async-start | bytes 1048576 | tf_op jit(solution)/shard_map/while/body/eval_jaxpr/all_to_all | solution.py:31
  393.5 5.2 copy-start.2
  393.5 5.1 collective-permute-start
  398.6 28.9 %copy-start = (bf16[2048,768]{1,0:T(8,128)(2,1)S(1)}, bf16[2048,768]{1,0:T(8,128)(2,1)}, u32[]{:S(2)}) copy-start(bf16[2048,768]{1,0:T(8,128)(2,1)} %get-tuple-element.514) | copy-start | bytes 9437188 | tf_op jit(solution)/shard_map/while
  430.0 13.0 %copy-start.1 = (bf16[1,2,16,2048]{3,2,1,0:T(8,128)(2,1)S(1)}, bf16[1,2,16,2048]{3,2,1,0:T(8,128)(2,1)}, u32[]{:S(2)}) copy-start(bf16[1,2,16,2048]{3,2,1,0:T(8,128)(2,1)} %get-tuple-element.492) | copy-start | bytes 393220 | tf_op jit(solution)/shard_map/while
  435.4 22.1 %all-to-all-start.1 = ((bf16[32,4,2048]{2,1,0:T(4,128)(2,1)}), bf16[32,4,2048]{2,1,0:T(4,128)(2,1)S(1)}, u32[]{:S(2)}, u32[]{:S(2)}) async-start(bf16[32,4,2048]{2,1,0:T(4,128)(2,1)} %reshape.112), calls=%async_computation.1 | async-start | bytes 1048576 | tf_op jit(solution)/shard_map/while/body/eval_jaxpr/all_to_all | solution.py:31
  458.1 5.2 copy-start.2
  458.2 5.1 collective-permute-start
  463.3 29.0 %copy-start = (bf16[2048,768]{1,0:T(8,128)(2,1)S(1)}, bf16[2048,768]{1,0:T(8,128)(2,1)}, u32[]{:S(2)}) copy-start(bf16[2048,768]{1,0:T(8,128)(2,1)} %get-tuple-element.514) | copy-start | bytes 9437188 | tf_op jit(solution)/shard_map/while
  494.6 13.0 %copy-start.1 = (bf16[1,2,16,2048]{3,2,1,0:T(8,128)(2,1)S(1)}, bf16[1,2,16,2048]{3,2,1,0:T(8,128)(2,1)}, u32[]{:S(2)}) copy-start(bf16[1,2,16,2048]{3,2,1,0:T(8,128)(2,1)} %get-tuple-element.492) | copy-start | bytes 393220 | tf_op jit(solution)/shard_map/while
  500.0 22.1 %all-to-all-start.1 = ((bf16[32,4,2048]{2,1,0:T(4,128)(2,1)}), bf16[32,4,2048]{2,1,0:T(4,128)(2,1)S(1)}, u32[]{:S(2)}, u32[]{:S(2)}) async-start(bf16[32,4,2048]{2,1,0:T(4,128)(2,1)} %reshape.112), calls=%async_computation.1 | async-start | bytes 1048576 | tf_op jit(solution)/shard_map/while/body/eval_jaxpr/all_to_all | solution.py:31
  522.8 5.2 copy-start.2
  522.8 5.1 collective-permute-start
  528.0 29.0 %copy-start = (bf16[2048,768]{1,0:T(8,128)(2,1)S(1)}, bf16[2048,768]{1,0:T(8,128)(2,1)}, u32[]{:S(2)}) copy-start(bf16[2048,768]{1,0:T(8,128)(2,1)} %get-tuple-element.514) | copy-start | bytes 9437188 | tf_op jit(solution)/shard_map/while
  559.3 13.0 %copy-start.1 = (bf16[1,2,16,2048]{3,2,1,0:T(8,128)(2,1)S(1)}, bf16[1,2,16,2048]{3,2,1,0:T(8,128)(2,1)}, u32[]{:S(2)}) copy-start(bf16[1,2,16,2048]{3,2,1,0:T(8,128)(2,1)} %get-tuple-element.492) | copy-start | bytes 393220 | tf_op jit(solution)/shard_map/while
  564.7 22.1 %all-to-all-start.1 = ((bf16[32,4,2048]{2,1,0:T(4,128)(2,1)}), bf16[32,4,2048]{2,1,0:T(4,128)(2,1)S(1)}, u32[]{:S(2)}, u32[]{:S(2)}) async-start(bf16[32,4,2048]{2,1,0:T(4,128)(2,1)} %reshape.112), calls=%async_computation.1 | async-start | bytes 1048576 | tf_op jit(solution)/shard_map/while/body/eval_jaxpr/all_to_all | solution.py:31
  587.5 5.2 copy-start.2
  587.5 5.1 collective-permute-start
where the time goes:
time: 596 us; the launch traced here: 593 us
  blocking collectives  188 us (32%)
  waiting for transfers between devices  153 us (26%)
  starting transfers between devices  94.7 us (16%)
  matrix products  78.3 us (13%)
  local copies, waits for them, and re-layouts  56.1 us (9%)
  other arithmetic  21.5 us (4%)
    all_to_all x9, blocking collectives, run_layer(): lax.all_to_all(copies, 'expert', split_axis=0, concat_axis=0, tiled=True)  188 us
    all_to_all x9, waiting for transfers between devices, return_rows(): lax.all_to_all(partial_value, 'expert', split_axis=0, concat_axis=0, tile...  131 us
    all_to_all x9, starting transfers between devices, return_rows(): lax.all_to_all(partial_value, 'expert', split_axis=0, concat_axis=0, tile...  61 us
    dot_general x9, matrix products, expert_rows(): jnp.dot(product, down_rows, preferred_element_type=jnp.float32)  39.7 us
    ppermute x9, starting transfers between devices, shifted(): return lax.ppermute(shard, axis, pairs)  33.7 us
    ppermute x9, waiting for transfers between devices, shifted(): return lax.ppermute(shard, axis, pairs)  21.7 us
    dot_general x9, matrix products, expert_rows(): gate_act = jnp.dot(flat_rows, gate_cols, preferred_element_type=jnp.float32)  21.4 us
    reshape x9, local copies, waits for them, and re-layouts, expert_rows(): flat_rows = arrived.reshape(-1, arrived.shape[-1])  17.5 us
  transfers between devices with their start and end apart: 18, of which 18 were waited for; matrix products, arithmetic and copies ran while one was open for 0% of the time, Pallas kernels for 0%

commit v1 on v0

v1 whole, which is shorter than its diff:
```python
import functools

import jax
import jax.numpy as jnp
from jax import lax
from jax.experimental import pallas as pl
from jax.experimental.pallas import tpu as pltpu
from jax.sharding import PartitionSpec as P

MESH = pl.DeviceIdType.MESH
CAP = 4
PIECES = 4
UNIT = CAP * PIECES
GROUP = 16
Z_SIZE = 8

F32 = jnp.float32
BF16 = jnp.bfloat16
I32 = jnp.int32


def iota(shape, dim):
    return lax.broadcasted_iota(I32, shape, dim)


def matmul(a, b):
    return jnp.dot(a, b, preferred_element_type=F32)


def matmul_nt(a, b):
    return lax.dot_general(a, b, (((1,), (1,)), ((), ())), preferred_element_type=F32)


def far_first(step, size):
    half = (step + 1) // 2
    return size // 2 + half * (1 - 2 * (step % 2))


def kernel(
    sections,
    devices,
    z_size,
    tokens_ref,
    gain_ref,
    gate_hbm,
    up_hbm,
    down_hbm,
    routes_ref,
    weights_ref,
    out_ref,
    gate_vm,
    up_vm,
    down_vm,
    x_vm,
    prev_vm,
    hid_vm,
    pack_vm,
    zmat_vm,
    mix_vm,
    mix_in,
    perm_vm,
    permt_vm,
    dsend,
    drecv,
    rsend,
    rrecv,
    arranged,
    act_vm,
    part_vm,
    w_sem,
    ds_sem,
    dr_sem,
    rs_sem,
    rr_sem,
    xs_sem,
    xr_sem,
    hs_sem,
    hr_sem,
    ms_sem,
    mr_sem,
):
    sec = lax.axis_index("section")
    me = lax.axis_index("expert")
    micro, tok, width = x_vm.shape
    part_w = width // PIECES
    experts = devices // 2
    slots = experts * CAP
    y_size = devices // z_size
    groups = devices // GROUP
    last = sections - 1
    first_sec = sec == 0
    last_sec = sec == last
    nxt = jnp.minimum(sec + 1, last)
    prv = jnp.maximum(sec - 1, 0)
    ret_base = micro * jnp.where(last_sec, 1, 0)

    weight_copies = [
        pltpu.make_async_copy(gate_hbm.at[0], gate_vm, w_sem.at[0]),
        pltpu.make_async_copy(up_hbm.at[0], up_vm, w_sem.at[1]),
        pltpu.make_async_copy(down_hbm.at[0], down_vm, w_sem.at[2]),
    ]
    for copy in weight_copies:
        copy.start()

    barrier = pltpu.get_barrier_semaphore()

    def greet_section(i, carry):
        pl.semaphore_signal(
            barrier, inc=1, device_id=(sec, lax.rem(me + i, devices)), device_id_type=MESH
        )
        return carry

    def greet_prev(i, carry):
        pl.semaphore_signal(
            barrier, inc=1, device_id=(prv, lax.rem(me + i, devices)), device_id_type=MESH
        )
        return carry

    lax.fori_loop(1, devices, greet_section, 0)

    @pl.when(jnp.logical_not(first_sec))
    def _():
        lax.fori_loop(0, devices, greet_prev, 0)

    @pl.when(jnp.logical_not(last_sec))
    def _():
        pl.semaphore_signal(barrier, inc=1, device_id=(nxt, me), device_id_type=MESH)

    def tables(m, carry):
        picked = routes_ref[0, m]
        share = weights_ref[0, m]
        choice = jnp.concatenate([picked[:, 0:1], picked[:, 1:2]], axis=0)
        scale = jnp.concatenate([share[:, 0:1], share[:, 1:2]], axis=0)
        count = 2 * tok
        onehot = (choice == iota((count, experts), 1)).astype(F32)
        below = (iota((count, count), 1) < iota((count, count), 0)).astype(BF16)
        earlier = matmul(below, onehot.astype(BF16))
        slot = jnp.sum(earlier * onehot, axis=1, keepdims=True).astype(I32)
        place = choice * CAP + slot
        hit = (place == iota((count, slots), 1)).astype(F32)
        index_row = iota((8, slots), 1).astype(BF16)
        row0 = matmul_nt(index_row, jnp.concatenate([hit[:tok]] * PIECES, axis=0).astype(BF16))
        row1 = matmul_nt(index_row, jnp.concatenate([hit[tok:]] * PIECES, axis=0).astype(BF16))
        shape = (experts * UNIT, PIECES * tok)
        r, c = iota(shape, 0), iota(shape, 1)
        want = (r // UNIT) * CAP + r % CAP
        same = (r // CAP) % PIECES == c // tok
        names = (row0[0:1].astype(I32) == want) | (row1[0:1].astype(I32) == want)
        pack_vm[m] = (names & same).astype(F32).astype(BF16)
        lane = iota((count, devices * CAP), 1)
        lands = (lane // (2 * CAP)) * CAP + lane % CAP == place
        weighted = jnp.where(lands, scale, 0.0)
        mix_vm[m] = weighted[:tok] + weighted[tok:]
        return carry

    def spread(mix, m):
        high = mix.astype(BF16)
        rest = mix - high.astype(F32)
        mid = rest.astype(BF16)
        low = (rest - mid.astype(F32)).astype(BF16)
        terms = jnp.concatenate([high, mid, low], axis=0)
        shape = (devices * CAP, devices * UNIT)
        j, c = iota(shape, 0), iota(shape, 1)
        widen = ((c // UNIT == j // CAP) & (c % CAP == j % CAP)).astype(F32).astype(BF16)
        wide = matmul(terms, widen)
        lane = iota((tok, devices * UNIT), 1)
        rows = []
        for term in range(3):
            block = wide[term * tok : (term + 1) * tok]
            for piece in range(PIECES):
                rows.append(jnp.where((lane // CAP) % PIECES == piece, block, 0.0))
        zmat_vm[m] = jnp.concatenate(rows, axis=0).astype(BF16)

    def permutations():
        size = GROUP * UNIT
        r, c = iota((size, size), 0), iota((size, size), 1)

        def moved(a, b):
            return (
                (a // (GROUP * CAP) == (b // CAP) % PIECES)
                & ((a // CAP) % GROUP == b // UNIT)
                & (a % CAP == b % CAP)
            )

        perm_vm[...] = moved(r, c).astype(F32).astype(BF16)
        permt_vm[...] = moved(c, r).astype(F32).astype(BF16)

    lax.fori_loop(0, micro, tables, 0)

    mix_copy = pltpu.make_async_remote_copy(
        src_ref=mix_vm,
        dst_ref=mix_in,
        send_sem=ms_sem,
        recv_sem=mr_sem,
        device_id=(nxt, me),
        device_id_type=MESH,
    )

    def pieces_of(value):
        return [value[:, k * part_w : (k + 1) * part_w] for k in range(PIECES)]

    def combine(m, base, x_pieces):
        total = matmul(zmat_vm[m], rrecv[base])
        rows = PIECES * tok
        summed = (total[2 * rows :] + total[rows : 2 * rows]) + total[:rows]
        return [
            (x_pieces[k].astype(F32) + summed[k * tok : (k + 1) * tok]).astype(BF16)
            for k in range(PIECES)
        ]

    def x_copy(m):
        return pltpu.make_async_remote_copy(
            src_ref=x_vm.at[m],
            dst_ref=prev_vm.at[m],
            send_sem=xs_sem.at[m],
            recv_sem=xr_sem.at[m],
            device_id=(nxt, me),
            device_id_type=MESH,
        )

    def hid_copy(m):
        return pltpu.make_async_remote_copy(
            src_ref=x_vm.at[m],
            dst_ref=hid_vm.at[m],
            send_sem=hs_sem.at[m],
            recv_sem=hr_sem.at[m],
            device_id=(prv, me),
            device_id_type=MESH,
        )

    def wait_block(buffer, sem):
        pltpu.make_async_copy(buffer, buffer, sem).wait()

    def target(i):
        y = lax.rem(me // z_size + far_first(i % y_size, y_size), y_size)
        z = lax.rem(me % z_size + far_first(i // y_size, z_size), z_size)
        return y * z_size + z

    def micro_batch(m, carry):
        @pl.when(first_sec)
        def _():
            x_vm[m] = tokens_ref[m]

        @pl.when(jnp.logical_not(first_sec))
        def _():
            @pl.when(m == 0)
            def _():
                wait_block(mix_in, mr_sem)

                def widen(k, carry):
                    spread(mix_in[k], k)
                    return carry

                lax.fori_loop(0, micro, widen, 0)

            wait_block(prev_vm.at[m], xr_sem.at[m])
            wait_block(rrecv.at[m], rr_sem.at[m])
            done = combine(m, m, pieces_of(prev_vm[m]))
            for k in range(PIECES):
                x_vm[m, :, k * part_w : (k + 1) * part_w] = done[k]

        wide = x_vm[m].astype(F32)
        mean = jnp.mean(wide * wide, axis=-1, keepdims=True)
        normed = (wide * lax.rsqrt(mean + 1e-06) * gain_ref[...]).astype(BF16)
        stacked = jnp.concatenate(pieces_of(normed), axis=0)
        dsend[m] = matmul(pack_vm[m], stacked).astype(BF16)

        def send_rows(i, carry):
            to = target(i)
            pltpu.make_async_remote_copy(
                src_ref=dsend.at[m, pl.ds(pl.multiple_of((to // 2) * UNIT, UNIT), UNIT)],
                dst_ref=drecv.at[m, pl.ds(pl.multiple_of(me * UNIT, UNIT), UNIT)],
                send_sem=ds_sem.at[m],
                recv_sem=dr_sem.at[m],
                device_id=(sec, to),
                device_id_type=MESH,
            ).start()
            return carry

        lax.fori_loop(0, devices - 1, send_rows, 0)
        pltpu.make_async_copy(
            dsend.at[m, pl.ds(pl.multiple_of((me // 2) * UNIT, UNIT), UNIT)],
            drecv.at[m, pl.ds(pl.multiple_of(me * UNIT, UNIT), UNIT)],
            dr_sem.at[m],
        ).start()

        @pl.when(jnp.logical_not(last_sec))
        def _():
            x_copy(m).start()

        @pl.when(jnp.logical_not(first_sec))
        def _():
            hid_copy(m).start()

        @pl.when(m == 0)
        def _():
            permutations()
            for copy in weight_copies:
                copy.wait()

        wait_block(drecv.at[m], dr_sem.at[m])
        span = GROUP * CAP
        for g in range(groups):
            rows = drecv[m, g * GROUP * UNIT : (g + 1) * GROUP * UNIT]
            moved = matmul(perm_vm[...], rows).astype(BF16)
            for k in range(PIECES):
                arranged[g * span : (g + 1) * span, k * part_w : (k + 1) * part_w] = moved[
                    k * span : (k + 1) * span
                ]
        hidden_w = gate_vm.shape[1]
        block_n = min(256, hidden_w)
        lhs = arranged[...]
        for n in range(hidden_w // block_n):
            cols = slice(n * block_n, (n + 1) * block_n)
            gate = matmul(lhs, gate_vm[:, cols])
            up = matmul(lhs, up_vm[:, cols])
            act_vm[:, cols] = (gate / (1.0 + jnp.exp(-gate)) * up).astype(BF16)
        act = act_vm[...]
        for k in range(PIECES):
            part = matmul(act, down_vm[:, k * part_w : (k + 1) * part_w]).astype(BF16)
            for g in range(groups):
                part_vm[g, k * span : (k + 1) * span] = part[g * span : (g + 1) * span]
        for g in range(groups):
            rsend[m, g * GROUP * UNIT : (g + 1) * GROUP * UNIT] = matmul(
                permt_vm[...], part_vm[g]
            ).astype(BF16)

        def send_parts(i, carry):
            to = target(i)
            pltpu.make_async_remote_copy(
                src_ref=rsend.at[m, pl.ds(pl.multiple_of(to * UNIT, UNIT), UNIT)],
                dst_ref=rrecv.at[m + ret_base, pl.ds(pl.multiple_of(me * UNIT, UNIT), UNIT)],
                send_sem=rs_sem.at[m],
                recv_sem=rr_sem.at[m + ret_base],
                device_id=(nxt, to),
                device_id_type=MESH,
            ).start()
            return carry

        lax.fori_loop(0, devices - 1, send_parts, 0)

        own = pl.ds(pl.multiple_of(me * UNIT, UNIT), UNIT)

        @pl.when(last_sec)
        def _():
            pltpu.make_async_copy(
                rsend.at[m, own], rrecv.at[m + micro, own], rr_sem.at[m + micro]
            ).start()

        @pl.when(jnp.logical_not(last_sec))
        def _():
            pltpu.make_async_remote_copy(
                src_ref=rsend.at[m, own],
                dst_ref=rrecv.at[m, own],
                send_sem=rs_sem.at[m],
                recv_sem=rr_sem.at[m],
                device_id=(nxt, me),
                device_id_type=MESH,
            ).start()

        return carry

    pl.semaphore_wait(
        barrier,
        devices - 1 + jnp.where(last_sec, 0, devices) + jnp.where(first_sec, 0, 1),
    )

    @pl.when(jnp.logical_not(last_sec))
    def _():
        mix_copy.start()

    lax.fori_loop(0, micro, micro_batch, 0)

    @pl.when(last_sec)
    def _():
        def finish(m, carry):
            spread(mix_vm[m], m)
            wait_block(rrecv.at[m + micro], rr_sem.at[m + micro])
            done = combine(m, m + micro, pieces_of(x_vm[m]))
            for k in range(PIECES):
                out_ref[0, m, :, k * part_w : (k + 1) * part_w] = done[k]
            return carry

        lax.fori_loop(0, micro, finish, 0)

    @pl.when(jnp.logical_not(last_sec))
    def _():
        mix_copy.wait_send()

        def receive(m, carry):
            wait_block(hid_vm.at[m], hr_sem.at[m])
            out_ref[0, m] = hid_vm[m]
            x_copy(m).wait_send()
            return carry

        lax.fori_loop(0, micro, receive, 0)

    def drain(m, carry):
        others = pl.ds(0, (devices - 1) * UNIT)
        wait_block(rrecv.at[0, others], ds_sem.at[m])
        wait_block(rrecv.at[0, others], rs_sem.at[m])

        @pl.when(jnp.logical_not(last_sec))
        def _():
            wait_block(rrecv.at[0, pl.ds(0, UNIT)], rs_sem.at[m])

        @pl.when(jnp.logical_not(first_sec))
        def _():
            hid_copy(m).wait_send()

        return carry

    lax.fori_loop(0, micro, drain, 0)


def solution(mesh):
    sections, devices = mesh.shape["section"], mesh.shape["expert"]
    z_size = min(Z_SIZE, devices // 2)

    def on_device(tokens, norm_gain, w_gate, w_up, w_down, routes, route_weights):
        micro, tok, width = tokens.shape
        hidden_w = w_gate.shape[2]
        part_w = width // PIECES
        vmem = pl.BlockSpec(memory_space=pltpu.VMEM)
        hbm = pl.BlockSpec(memory_space=pl.ANY)
        block = (devices * UNIT, part_w)
        span = GROUP * UNIT
        dma = pltpu.SemaphoreType.DMA
        return pl.pallas_call(
            functools.partial(kernel, sections, devices, z_size),
            out_shape=jax.ShapeDtypeStruct((1, micro, tok, width), BF16),
            in_specs=[vmem, vmem, hbm, hbm, hbm, vmem, vmem],
            out_specs=vmem,
            scratch_shapes=[
                pltpu.VMEM((width, hidden_w), BF16),
                pltpu.VMEM((width, hidden_w), BF16),
                pltpu.VMEM((hidden_w, width), BF16),
                pltpu.VMEM((micro, tok, width), BF16),
                pltpu.VMEM((micro, tok, width), BF16),
                pltpu.VMEM((micro, tok, width), BF16),
                pltpu.VMEM((micro, devices // 2 * UNIT, PIECES * tok), BF16),
                pltpu.VMEM((micro, 3 * PIECES * tok, devices * UNIT), BF16),
                pltpu.VMEM((micro, tok, devices * CAP), F32),
                pltpu.VMEM((micro, tok, devices * CAP), F32),
                pltpu.VMEM((span, span), BF16),
                pltpu.VMEM((span, span), BF16),
                pltpu.VMEM((micro, devices // 2 * UNIT, part_w), BF16),
                pltpu.VMEM((micro,) + block, BF16),
                pltpu.VMEM((micro,) + block, BF16),
                pltpu.VMEM((2 * micro,) + block, BF16),
                pltpu.VMEM((devices * CAP, width), BF16),
                pltpu.VMEM((devices * CAP, hidden_w), BF16),
                pltpu.VMEM((devices // GROUP, span, part_w), BF16),
                dma((3,)),
                dma((micro,)),
                dma((micro,)),
                dma((micro,)),
                dma((2 * micro,)),
                dma((micro,)),
                dma((micro,)),
                dma((micro,)),
                dma((micro,)),
                dma,
                dma,
            ],
            compiler_params=pltpu.CompilerParams(
                collective_id=0, has_side_effects=True, vmem_limit_bytes=56 << 20
            ),
        )(tokens, norm_gain, w_gate, w_up, w_down, routes, route_weights)

    in_specs = (
        P(None, "expert", None),
        P("section", None),
        P("section", None, "expert"),
        P("section", None, "expert"),
        P("section", "expert", None),
        P("section", None, "expert", None),
        P("section", None, "expert", None),
    )
    return jax.shard_map(
        on_device,
        mesh=mesh,
        in_specs=in_specs,
        out_specs=P("section", None, "expert", None),
        check_vma=False,
    )
```

time: 596 us -> 241 us (0.40)
  the two profiles are of different devices: /device:TPU:1 before, /device:TPU:7 now
where the time goes in v1:
time: 241 us
  Pallas kernels  237 us (98%)
  local copies, waits for them, and re-layouts  4.29 us (2%)
    pallas_call x1, Pallas kernels, on_device(): pl.pallas_call(functools.partial(kernel, sections, devices, z_size), out_...  237 us

profile of v1, /device:TPU:7, one launch (start us, length us, event | category | flops | bytes accessed | tf_op | source)
XLA Modules:
  0.0 240.8 jit_solution(9436343577974003600)
XLA Ops:
  0.0 1.4 copy.8.routes_ref
  1.4 1.4 copy.9.weights_ref
  2.7 236.5 %shard_map.73 = bf16[1,2,16,2048]{3,2,1,0:T(8,128)(2,1)} custom-call(bf16[2,16,2048]{2,1,0:T(8,128)(2,1)} %tokens_ref.1, f32[1,2048]{1,0:T(1,128)} %gain_ref.1, bf16[1,2048,768]{2,1,0:T(8,128)(2,1)} %gate_hbm.1, bf16[1,2048,768]{2,1,0:T(8,128)(2,1)} %up_hbm.1, bf16[1,768,2048]{2,1,0:T(8,128)(2,1)} %down_hbm.1, s32[1,2,16,2]{3,2,1,0:T(8,128)} %copy.8.routes_ref, ...), custom_call_target="tpu_custom_call" | custom-call | tf_op jit(solution)/shard_map/pallas_call | solution.py:429
  239.3 1.6 copy.11

commit v2 on v1

--- a/solution.py
+++ b/solution.py
@@ -55,6 +55,8 @@
     prev_vm,
     hid_vm,
     pack_vm,
+    pack_in,
+    gain_in,
     zmat_vm,
     mix_vm,
     mix_in,
@@ -78,6 +80,8 @@
     hr_sem,
     ms_sem,
     mr_sem,
+    ps_sem,
+    pr_sem,
 ):
     sec = lax.axis_index("section")
     me = lax.axis_index("expert")
@@ -90,9 +94,15 @@
     last = sections - 1
     first_sec = sec == 0
     last_sec = sec == last
+
+    def home1(layer):
+        return lax.rem(layer + sections - 2 + 4 * lax.rem(layer, 2), sections)
+
+    hosted = lax.rem(sec + sections + 2 - 4 * lax.rem(sec, 2), sections)
     nxt = jnp.minimum(sec + 1, last)
     prv = jnp.maximum(sec - 1, 0)
-    ret_base = micro * jnp.where(last_sec, 1, 0)
+    nxt1 = jnp.where(last_sec, last, home1(nxt))
+    ret_base = jnp.where(last_sec, micro, 0)
 
     weight_copies = [
         pltpu.make_async_copy(gate_hbm.at[0], gate_vm, w_sem.at[0]),
@@ -104,27 +114,37 @@
 
     barrier = pltpu.get_barrier_semaphore()
 
-    def greet_section(i, carry):
-        pl.semaphore_signal(
-            barrier, inc=1, device_id=(sec, lax.rem(me + i, devices)), device_id_type=MESH
-        )
-        return carry
-
-    def greet_prev(i, carry):
-        pl.semaphore_signal(
-            barrier, inc=1, device_id=(prv, lax.rem(me + i, devices)), device_id_type=MESH
-        )
-        return carry
-
-    lax.fori_loop(1, devices, greet_section, 0)
+    def greet(section, device):
+        pl.semaphore_signal(barrier, inc=1, device_id=(section, device), device_id_type=MESH)
+
+    def greet_all(section, start):
+        def step(i, carry):
+            greet(section, lax.rem(me + i, devices))
+            return carry
+
+        lax.fori_loop(start, devices, step, 0)
+
+    greet_all(sec, 1)
+    greet_all(home1(sec), 0)
+    greet(hosted, me)
 
     @pl.when(jnp.logical_not(first_sec))
     def _():
-        lax.fori_loop(0, devices, greet_prev, 0)
+        greet_all(prv, 0)
+
+    @pl.when(hosted > 0)
+    def _():
+        greet_all(hosted - 1, 0)
+        greet(home1(hosted - 1), me)
 
     @pl.when(jnp.logical_not(last_sec))
     def _():
-        pl.semaphore_signal(barrier, inc=1, device_id=(nxt, me), device_id_type=MESH)
+        greet(nxt, me)
+        greet(nxt1, me)
+
+    @pl.when(last_sec)
+    def _():
+        greet(home1(last), me)
 
     def tables(m, carry):
         picked = routes_ref[0, m]
@@ -187,20 +207,64 @@
 
     lax.fori_loop(0, micro, tables, 0)
 
-    mix_copy = pltpu.make_async_remote_copy(
-        src_ref=mix_vm,
-        dst_ref=mix_in,
-        send_sem=ms_sem,
-        recv_sem=mr_sem,
-        device_id=(nxt, me),
-        device_id_type=MESH,
+    def send(src, dst, send_sem, recv_sem, section, device):
+        return pltpu.make_async_remote_copy(
+            src_ref=src,
+            dst_ref=dst,
+            send_sem=send_sem,
+            recv_sem=recv_sem,
+            device_id=(section, device),
+            device_id_type=MESH,
+        )
+
+    pl.semaphore_wait(
+        barrier,
+        2 * devices
+        + 1
+        + jnp.where(last_sec, 0, 2 * devices)
+        + jnp.where(first_sec, 0, 1)
+        + jnp.where(hosted == 0, 0, 1),
     )
+
+    x_to = [nxt, jnp.where(hosted == last, last, home1(jnp.minimum(hosted + 1, last)))]
+    x_slot = [0, jnp.where(hosted == last, micro, 1)]
+    hid_to = [prv, jnp.maximum(hosted - 1, 0)]
+    layer_of = [sec, hosted]
+
+    def x_copy(m):
+        return send(
+            x_vm.at[m], prev_vm.at[x_slot[m]], xs_sem.at[m], xr_sem.at[x_slot[m]], x_to[m], me
+        )
+
+    def hid_copy(m):
+        return send(x_vm.at[m], hid_vm.at[m], hs_sem.at[m], hr_sem.at[m], hid_to[m], me)
+
+    def mix_copy(m, to):
+        return send(mix_vm.at[m], mix_in.at[m], ms_sem.at[m], mr_sem.at[m], to, me)
+
+    def pack_copy():
+        return send(pack_vm.at[1], pack_in, ps_sem.at[0], pr_sem.at[0], home1(sec), me)
+
+    def gain_copy():
+        return send(gain_ref, gain_in, ps_sem.at[1], pr_sem.at[1], home1(sec), me)
+
+    def wait_block(buffer, sem):
+        pltpu.make_async_copy(buffer, buffer, sem).wait()
+
+    def hand_out_tables():
+        pack_copy().start()
+        gain_copy().start()
+
+        @pl.when(jnp.logical_not(last_sec))
+        def _():
+            mix_copy(0, nxt).start()
+            mix_copy(1, nxt1).start()
 
     def pieces_of(value):
         return [value[:, k * part_w : (k + 1) * part_w] for k in range(PIECES)]
 
-    def combine(m, base, x_pieces):
-        total = matmul(zmat_vm[m], rrecv[base])
+    def combine(z, base, x_pieces):
+        total = matmul(zmat_vm[z], rrecv[base])
         rows = PIECES * tok
         summed = (total[2 * rows :] + total[rows : 2 * rows]) + total[:rows]
         return [
@@ -208,93 +272,74 @@
             for k in range(PIECES)
         ]
 
-    def x_copy(m):
-        return pltpu.make_async_remote_copy(
-            src_ref=x_vm.at[m],
-            dst_ref=prev_vm.at[m],
-            send_sem=xs_sem.at[m],
-            recv_sem=xr_sem.at[m],
-            device_id=(nxt, me),
-            device_id_type=MESH,
-        )
-
-    def hid_copy(m):
-        return pltpu.make_async_remote_copy(
-            src_ref=x_vm.at[m],
-            dst_ref=hid_vm.at[m],
-            send_sem=hs_sem.at[m],
-            recv_sem=hr_sem.at[m],
-            device_id=(prv, me),
-            device_id_type=MESH,
-        )
-
-    def wait_block(buffer, sem):
-        pltpu.make_async_copy(buffer, buffer, sem).wait()
-
     def target(i):
         y = lax.rem(me // z_size + far_first(i % y_size, y_size), y_size)
         z = lax.rem(me % z_size + far_first(i // y_size, z_size), z_size)
         return y * z_size + z
 
-    def micro_batch(m, carry):
-        @pl.when(first_sec)
+    def block(index):
+        return pl.ds(pl.multiple_of(index * UNIT, UNIT), UNIT)
+
+    own = block(me)
+
+    def home(m):
+        layer = layer_of[m]
+
+        @pl.when(layer == 0)
         def _():
             x_vm[m] = tokens_ref[m]
 
-        @pl.when(jnp.logical_not(first_sec))
-        def _():
-            @pl.when(m == 0)
-            def _():
-                wait_block(mix_in, mr_sem)
-
-                def widen(k, carry):
-                    spread(mix_in[k], k)
-                    return carry
-
-                lax.fori_loop(0, micro, widen, 0)
-
+        @pl.when(layer > 0)
+        def _():
+            wait_block(mix_in.at[m], mr_sem.at[m])
+            spread(mix_in[m], m)
             wait_block(prev_vm.at[m], xr_sem.at[m])
             wait_block(rrecv.at[m], rr_sem.at[m])
             done = combine(m, m, pieces_of(prev_vm[m]))
             for k in range(PIECES):
                 x_vm[m, :, k * part_w : (k + 1) * part_w] = done[k]
 
+        if m == 0:
+            gain, pack = gain_ref[...], pack_vm[0]
+        else:
+            wait_block(pack_in, pr_sem.at[0])
+            wait_block(gain_in, pr_sem.at[1])
+            gain, pack = gain_in[...], pack_in[...]
         wide = x_vm[m].astype(F32)
         mean = jnp.mean(wide * wide, axis=-1, keepdims=True)
-        normed = (wide * lax.rsqrt(mean + 1e-06) * gain_ref[...]).astype(BF16)
+        normed = (wide * lax.rsqrt(mean + 1e-06) * gain).astype(BF16)
         stacked = jnp.concatenate(pieces_of(normed), axis=0)
-        dsend[m] = matmul(pack_vm[m], stacked).astype(BF16)
+        dsend[m] = matmul(pack, stacked).astype(BF16)
 
         def send_rows(i, carry):
             to = target(i)
-            pltpu.make_async_remote_copy(
-                src_ref=dsend.at[m, pl.ds(pl.multiple_of((to // 2) * UNIT, UNIT), UNIT)],
-                dst_ref=drecv.at[m, pl.ds(pl.multiple_of(me * UNIT, UNIT), UNIT)],
-                send_sem=ds_sem.at[m],
-                recv_sem=dr_sem.at[m],
-                device_id=(sec, to),
-                device_id_type=MESH,
+            send(
+                dsend.at[m, block(to // 2)],
+                drecv.at[m, own],
+                ds_sem.at[m],
+                dr_sem.at[m],
+                layer,
+                to,
             ).start()
             return carry
 
-        lax.fori_loop(0, devices - 1, send_rows, 0)
-        pltpu.make_async_copy(
-            dsend.at[m, pl.ds(pl.multiple_of((me // 2) * UNIT, UNIT), UNIT)],
-            drecv.at[m, pl.ds(pl.multiple_of(me * UNIT, UNIT), UNIT)],
-            dr_sem.at[m],
-        ).start()
-
-        @pl.when(jnp.logical_not(last_sec))
+        lax.fori_loop(0, devices - 1 + m, send_rows, 0)
+        if m == 0:
+            pltpu.make_async_copy(
+                dsend.at[m, block(me // 2)], drecv.at[m, own], dr_sem.at[m]
+            ).start()
+
+        @pl.when(layer < last if m == 0 else layer >= 0)
         def _():
             x_copy(m).start()
 
-        @pl.when(jnp.logical_not(first_sec))
+        @pl.when(layer > 0)
         def _():
             hid_copy(m).start()
 
+    def expert(m, carry):
         @pl.when(m == 0)
         def _():
-            permutations()
             for copy in weight_copies:
                 copy.wait()
 
@@ -325,92 +370,94 @@
                 permt_vm[...], part_vm[g]
             ).astype(BF16)
 
+        section = jnp.where(m == 0, nxt, nxt1)
+        slot = m + ret_base
+
         def send_parts(i, carry):
             to = target(i)
-            pltpu.make_async_remote_copy(
-                src_ref=rsend.at[m, pl.ds(pl.multiple_of(to * UNIT, UNIT), UNIT)],
-                dst_ref=rrecv.at[m + ret_base, pl.ds(pl.multiple_of(me * UNIT, UNIT), UNIT)],
-                send_sem=rs_sem.at[m],
-                recv_sem=rr_sem.at[m + ret_base],
-                device_id=(nxt, to),
-                device_id_type=MESH,
+            send(
+                rsend.at[m, block(to)],
+                rrecv.at[slot, own],
+                rs_sem.at[m],
+                rr_sem.at[slot],
+                section,
+                to,
             ).start()
             return carry
 
-        lax.fori_loop(0, devices - 1, send_parts, 0)
-
-        own = pl.ds(pl.multiple_of(me * UNIT, UNIT), UNIT)
+        lax.fori_loop(0, devices - jnp.where(last_sec, 1, 0), send_parts, 0)
 
         @pl.when(last_sec)
         def _():
-            pltpu.make_async_copy(
-                rsend.at[m, own], rrecv.at[m + micro, own], rr_sem.at[m + micro]
-            ).start()
-
-        @pl.when(jnp.logical_not(last_sec))
-        def _():
-            pltpu.make_async_remote_copy(
-                src_ref=rsend.at[m, own],
-                dst_ref=rrecv.at[m, own],
-                send_sem=rs_sem.at[m],
-                recv_sem=rr_sem.at[m],
-                device_id=(nxt, me),
-                device_id_type=MESH,
-            ).start()
+            pltpu.make_async_copy(rsend.at[m, own], rrecv.at[slot, own], rr_sem.at[slot]).start()
 
         return carry
 
-    pl.semaphore_wait(
-        barrier,
-        devices - 1 + jnp.where(last_sec, 0, devices) + jnp.where(first_sec, 0, 1),
-    )
-
-    @pl.when(jnp.logical_not(last_sec))
-    def _():
-        mix_copy.start()
-
-    lax.fori_loop(0, micro, micro_batch, 0)
+    early = ((lax.rem(sec, 2) == 1) & (hosted < last)) | (hosted == 0)
+
+    @pl.when(first_sec)
+    def _():
+        home(0)
+        hand_out_tables()
+        permutations()
+
+    @pl.when(jnp.logical_not(first_sec))
+    def _():
+        hand_out_tables()
+        permutations()
+
+    @pl.when(early)
+    def _():
+        home(1)
+
+    @pl.when(jnp.logical_not(first_sec))
+    def _():
+        home(0)
+
+    lax.fori_loop(0, micro, expert, 0)
+
+    @pl.when(jnp.logical_not(early))
+    def _():
+        home(1)
 
     @pl.when(last_sec)
     def _():
-        def finish(m, carry):
+        wait_block(prev_vm.at[micro], xr_sem.at[micro])
+        for m in range(micro):
             spread(mix_vm[m], m)
             wait_block(rrecv.at[m + micro], rr_sem.at[m + micro])
-            done = combine(m, m + micro, pieces_of(x_vm[m]))
+            x_ref = x_vm.at[0] if m == 0 else prev_vm.at[micro]
+            done = combine(m, m + micro, pieces_of(x_ref[...]))
             for k in range(PIECES):
                 out_ref[0, m, :, k * part_w : (k + 1) * part_w] = done[k]
-            return carry
-
-        lax.fori_loop(0, micro, finish, 0)
 
     @pl.when(jnp.logical_not(last_sec))
     def _():
-        mix_copy.wait_send()
-
-        def receive(m, carry):
+        mix_copy(0, nxt).wait_send()
+        mix_copy(1, nxt1).wait_send()
+        x_copy(0).wait_send()
+        for m in range(micro):
             wait_block(hid_vm.at[m], hr_sem.at[m])
             out_ref[0, m] = hid_vm[m]
-            x_copy(m).wait_send()
-            return carry
-
-        lax.fori_loop(0, micro, receive, 0)
-
-    def drain(m, carry):
-        others = pl.ds(0, (devices - 1) * UNIT)
-        wait_block(rrecv.at[0, others], ds_sem.at[m])
-        wait_block(rrecv.at[0, others], rs_sem.at[m])
+
+    pack_copy().wait_send()
+    gain_copy().wait_send()
+    x_copy(1).wait_send()
+    most = pl.ds(0, (devices - 1) * UNIT)
+    one = pl.ds(0, UNIT)
+    for m in range(micro):
+        wait_block(rrecv.at[0, most], ds_sem.at[m])
+        wait_block(rrecv.at[0, most], rs_sem.at[m])
 
         @pl.when(jnp.logical_not(last_sec))
         def _():
-            wait_block(rrecv.at[0, pl.ds(0, UNIT)], rs_sem.at[m])
-
-        @pl.when(jnp.logical_not(first_sec))
+            wait_block(rrecv.at[0, one], rs_sem.at[m])
+
+        @pl.when(layer_of[m] > 0)
         def _():
             hid_copy(m).wait_send()
 
-        return carry
-
-    lax.fori_loop(0, micro, drain, 0)
+    wait_block(rrecv.at[0, one], ds_sem.at[1])
 
 
 def solution(mesh):
@@ -436,9 +483,11 @@
                 pltpu.VMEM((width, hidden_w), BF16),
                 pltpu.VMEM((hidden_w, width), BF16),
                 pltpu.VMEM((micro, tok, width), BF16),
-                pltpu.VMEM((micro, tok, width), BF16),
+                pltpu.VMEM((micro + 1, tok, width), BF16),
                 pltpu.VMEM((micro, tok, width), BF16),
                 pltpu.VMEM((micro, devices // 2 * UNIT, PIECES * tok), BF16),
+                pltpu.VMEM((devices // 2 * UNIT, PIECES * tok), BF16),
+                pltpu.VMEM((1, width), F32),
                 pltpu.VMEM((micro, 3 * PIECES * tok, devices * UNIT), BF16),
                 pltpu.VMEM((micro, tok, devices * CAP), F32),
                 pltpu.VMEM((micro, tok, devices * CAP), F32),
@@ -457,11 +506,13 @@
                 dma((micro,)),
                 dma((2 * micro,)),
                 dma((micro,)),
-                dma((micro,)),
-                dma((micro,)),
-                dma((micro,)),
-                dma,
-                dma,
+                dma((micro + 1,)),
+                dma((micro,)),
+                dma((micro,)),
+                dma((micro,)),
+                dma((micro,)),
+                dma((2,)),
+                dma((2,)),
             ],
             compiler_params=pltpu.CompilerParams(
                 collective_id=0, has_side_effects=True, vmem_limit_bytes=56 << 20

time: 241 us -> 219 us (0.909)
  Pallas kernels: 237 us -> 215 us
    pallas_call x1, Pallas kernels: 237 us -> 215 us  [on_device(): pl.pallas_call(functools.partial(kernel, sections, devices, z_size), out_...]
where the time goes in v2:
time: 219 us
  Pallas kernels  215 us (98%)
  local copies, waits for them, and re-layouts  4.29 us (2%)
    pallas_call x1, Pallas kernels, on_device(): pl.pallas_call(functools.partial(kernel, sections, devices, z_size), out_...  215 us

profile of v2, /device:TPU:7, one launch (start us, length us, event | category | flops | bytes accessed | tf_op | source)
XLA Modules:
  0.0 219.2 jit_solution(11883812595097044952)
XLA Ops:
  0.0 1.4 copy.8.routes_ref
  1.4 1.4 copy.9.weights_ref
  2.7 214.9 %shard_map.73 = bf16[1,2,16,2048]{3,2,1,0:T(8,128)(2,1)} custom-call(bf16[2,16,2048]{2,1,0:T(8,128)(2,1)} %tokens_ref.1, f32[1,2048]{1,0:T(1,128)} %gain_ref.1, bf16[1,2048,768]{2,1,0:T(8,128)(2,1)} %gate_hbm.1, bf16[1,2048,768]{2,1,0:T(8,128)(2,1)} %up_hbm.1, bf16[1,768,2048]{2,1,0:T(8,128)(2,1)} %down_hbm.1, s32[1,2,16,2]{3,2,1,0:T(8,128)} %copy.8.routes_ref, ...), custom_call_target="tpu_custom_call" | custom-call | tf_op jit(solution)/shard_map/pallas_call | solution.py:476
  217.7 1.6 copy.11

commit v3 on v2

--- a/solution.py
+++ b/solution.py
@@ -117,24 +117,23 @@
     def greet(section, device):
         pl.semaphore_signal(barrier, inc=1, device_id=(section, device), device_id_type=MESH)
 
-    def greet_all(section, start):
+    greet(hosted, me)
+
+    @pl.when(first_sec)
+    def _():
         def step(i, carry):
-            greet(section, lax.rem(me + i, devices))
+            greet(sec, lax.rem(me + i, devices))
             return carry
 
-        lax.fori_loop(start, devices, step, 0)
-
-    greet_all(sec, 1)
-    greet_all(home1(sec), 0)
-    greet(hosted, me)
+        lax.fori_loop(1, devices, step, 0)
 
     @pl.when(jnp.logical_not(first_sec))
     def _():
-        greet_all(prv, 0)
+        greet(prv, me)
 
     @pl.when(hosted > 0)
     def _():
-        greet_all(hosted - 1, 0)
+        greet(hosted - 1, me)
         greet(home1(hosted - 1), me)
 
     @pl.when(jnp.logical_not(last_sec))
@@ -219,12 +218,12 @@
 
     pl.semaphore_wait(
         barrier,
-        2 * devices
-        + 1
-        + jnp.where(last_sec, 0, 2 * devices)
-        + jnp.where(first_sec, 0, 1)
-        + jnp.where(hosted == 0, 0, 1),
+        4 + jnp.where(first_sec, devices - 2, 0) + jnp.where(last_sec, 0, 2),
     )
+
+    @pl.when(first_sec)
+    def _():
+        greet(home1(sec), me)
 
     x_to = [nxt, jnp.where(hosted == last, last, home1(jnp.minimum(hosted + 1, last)))]
     x_slot = [0, jnp.where(hosted == last, micro, 1)]
@@ -311,7 +310,7 @@
         stacked = jnp.concatenate(pieces_of(normed), axis=0)
         dsend[m] = matmul(pack, stacked).astype(BF16)
 
-        def send_rows(i, carry):
+        def send_rows(i):
             to = target(i)
             send(
                 dsend.at[m, block(to // 2)],
@@ -321,9 +320,9 @@
                 layer,
                 to,
             ).start()
-            return carry
-
-        lax.fori_loop(0, devices - 1 + m, send_rows, 0)
+
+        for i in range(devices - 1 + m):
+            send_rows(i)
         if m == 0:
             pltpu.make_async_copy(
                 dsend.at[m, block(me // 2)], drecv.at[m, own], dr_sem.at[m]
@@ -373,7 +372,7 @@
         section = jnp.where(m == 0, nxt, nxt1)
         slot = m + ret_base
 
-        def send_parts(i, carry):
+        def send_parts(i):
             to = target(i)
             send(
                 rsend.at[m, block(to)],
@@ -383,9 +382,13 @@
                 section,
                 to,
             ).start()
-            return carry
-
-        lax.fori_loop(0, devices - jnp.where(last_sec, 1, 0), send_parts, 0)
+
+        for i in range(devices - 1):
+            send_parts(i)
+
+        @pl.when(jnp.logical_not(last_sec))
+        def _():
+            send_parts(devices - 1)
 
         @pl.when(last_sec)
         def _():

time: 219 us -> 214 us (0.977)
  Pallas kernels: 215 us -> 209 us
    pallas_call x1, Pallas kernels: 215 us -> 209 us  [on_device(): pl.pallas_call(functools.partial(kernel, sections, devices, z_size), out_...]
where the time goes in v3:
time: 214 us; the launch traced here: 213 us
  Pallas kernels  209 us (98%)
  local copies, waits for them, and re-layouts  4.29 us (2%)
    pallas_call x1, Pallas kernels, on_device(): pl.pallas_call(functools.partial(kernel, sections, devices, z_size), out_...  209 us
    unnamed x3, local copies, waits for them, and re-layouts  4.29 us

profile of v3, /device:TPU:7, one launch (start us, length us, event | category | flops | bytes accessed | tf_op | source)
XLA Modules:
  0.0 213.4 jit_solution(9237893400443276654)
XLA Ops:
  0.0 1.4 copy.8.routes_ref
  1.4 1.4 copy.9.weights_ref
  2.7 209.1 %shard_map.73 = bf16[1,2,16,2048]{3,2,1,0:T(8,128)(2,1)} custom-call(bf16[2,16,2048]{2,1,0:T(8,128)(2,1)} %tokens_ref.1, f32[1,2048]{1,0:T(1,128)} %gain_ref.1, bf16[1,2048,768]{2,1,0:T(8,128)(2,1)} %gate_hbm.1, bf16[1,2048,768]{2,1,0:T(8,128)(2,1)} %up_hbm.1, bf16[1,768,2048]{2,1,0:T(8,128)(2,1)} %down_hbm.1, s32[1,2,16,2]{3,2,1,0:T(8,128)} %copy.8.routes_ref, ...), custom_call_target="tpu_custom_call" | custom-call | tf_op jit(solution)/shard_map/pallas_call | solution.py:479
  211.8 1.6 copy.11

commit v4 on v3

--- a/solution.py
+++ b/solution.py
@@ -271,10 +271,15 @@
             for k in range(PIECES)
         ]
 
+    def hops(step, size):
+        return min(step, size - step)
+
+    offsets = [(dy, dz) for dy in range(y_size) for dz in range(z_size)]
+    offsets.sort(key=lambda o: (-hops(o[1], z_size) - hops(o[0], y_size), -hops(o[1], z_size), o[0], o[1]))
+
     def target(i):
-        y = lax.rem(me // z_size + far_first(i % y_size, y_size), y_size)
-        z = lax.rem(me % z_size + far_first(i // y_size, z_size), z_size)
-        return y * z_size + z
+        dy, dz = offsets[i]
+        return lax.rem(me // z_size + dy, y_size) * z_size + lax.rem(me % z_size + dz, z_size)
 
     def block(index):
         return pl.ds(pl.multiple_of(index * UNIT, UNIT), UNIT)

time: 214 us -> 212 us (level)
  no operation moved by 1% of the time
where the time goes in v4:
time: 212 us
  Pallas kernels  207 us (98%)
  local copies, waits for them, and re-layouts  4.29 us (2%)
    pallas_call x1, Pallas kernels, on_device(): pl.pallas_call(functools.partial(kernel, sections, devices, z_size), out_...  207 us
    unnamed x3, local copies, waits for them, and re-layouts  4.29 us

profile of v4, /device:TPU:7, one launch (start us, length us, event | category | flops | bytes accessed | tf_op | source)
XLA Modules:
  0.0 211.5 jit_solution(2877090744458920600)
XLA Ops:
  0.0 1.4 copy.8.routes_ref
  1.4 1.4 copy.9.weights_ref
  2.7 207.2 %shard_map.73 = bf16[1,2,16,2048]{3,2,1,0:T(8,128)(2,1)} custom-call(bf16[2,16,2048]{2,1,0:T(8,128)(2,1)} %tokens_ref.1, f32[1,2048]{1,0:T(1,128)} %gain_ref.1, bf16[1,2048,768]{2,1,0:T(8,128)(2,1)} %gate_hbm.1, bf16[1,2048,768]{2,1,0:T(8,128)(2,1)} %up_hbm.1, bf16[1,768,2048]{2,1,0:T(8,128)(2,1)} %down_hbm.1, s32[1,2,16,2]{3,2,1,0:T(8,128)} %copy.8.routes_ref, ...), custom_call_target="tpu_custom_call" | custom-call | tf_op jit(solution)/shard_map/pallas_call | solution.py:484
  209.9 1.6 copy.11
